TPU v7x, 32 devices: a whole 2x2x4 slice. The times are simulated.
32 devices in a mesh: seq: 4 (over x, core), chan: 8 (over z, y).
Axes of the slice: x: 2, y: 2, z: 4, core: 2. Of those that a mesh axis runs over, the one named last changes fastest.
Arguments:
- d_out: bfloat16 [2048, 8192], P('seq', 'chan'), may hold values from -6 to 6
- w_out: bfloat16 [1024, 8192], P('chan'), may hold values from -0.0625 to 0.0625
- gate: bfloat16 [2048, 1024], P('seq', 'chan'), may hold values from -6 to 6
- inner: bfloat16 [2048, 1024], P('seq', 'chan'), may hold values from -0.125 to 0.125
- filt: bfloat16 [2048, 1024], P('seq', 'chan'), may hold values from -4 to 4
Outputs:
- grad_inner: bfloat16 [2048, 1024], P('seq', 'chan')
- grad_filter: float32 [2048, 1024], P('seq', 'chan')
All inputs are finite; a program needn't handle non-finite values.
Results may differ from a plain program's by a relative error of at most 0.005.
Values may be sent and summed in bfloat16 or wider, within the bound.
No kernel may reach another device: no remote copies, remote signals or barrier semaphores. Data moves between devices by JAX's collectives and lax.ppermute only.
A program may use at most 64 MiB of HBM per device.

v0:
```python
import math
import jax
import jax.numpy as jnp
from jax import lax
from jax.sharding import PartitionSpec as P

SUBS = 4


def spread(block, axis, holder):
    block = jnp.where(lax.axis_index(axis) == holder, block, jnp.zeros_like(block))
    return lax.psum(block, axis)


def shifted(block, axis, distance):
    devices = range(lax.axis_size(axis))
    route = [(i - distance, i) for i in devices if i - distance in devices]
    return lax.ppermute(block, axis, route)


def split_pair(matrix_in):
    upper = lax.optimization_barrier(matrix_in.astype(jnp.bfloat16))
    lower = (matrix_in - upper.astype(jnp.float32)).astype(jnp.bfloat16)
    return (upper, lower)


def body(d_out, w_out, gate, inner, filt):
    block_rows, channels = gate.shape
    sub_rows = block_rows // SUBS
    size_n = 2 * sub_rows
    seq_count = lax.axis_size("seq")
    grad_gated = jnp.einsum(
        "td,cd->tc",
        lax.all_gather(d_out, "chan", axis=1, tiled=True),
        w_out,
        preferred_element_type=jnp.float32,
    )
    grad_conv = (gate.astype(jnp.float32) * grad_gated).astype(jnp.bfloat16)
    index_row = jnp.arange(sub_rows, dtype=jnp.int32)
    angles = (index_row[:, None] * index_row[None, :] % size_n).astype(jnp.float32) * (
        2.0 * math.pi / size_n
    )
    alternate = (1 - 2 * (index_row % 2)).astype(jnp.float32)
    sine_part = (-jnp.sin(angles)).at[0].set(alternate)
    forward_upper, forward_lower = split_pair(jnp.concatenate([jnp.cos(angles), sine_part], axis=0))
    weights = jnp.where(index_row == 0, 1.0, 2.0).astype(jnp.float32)[None, :] / size_n
    inverse_sines = (-2.0 * jnp.sin(angles) / size_n).at[:, 0].set(alternate / size_n)
    inverse_matrix = jnp.concatenate([jnp.cos(angles) * weights, inverse_sines], axis=1)
    nyquist_sign = jnp.full((1,), float(1 - 2 * (sub_rows % 2)), jnp.float32)
    parity = jnp.concatenate([alternate, nyquist_sign, alternate[1:]])[:, None]
    conj_sign = jnp.concatenate(
        [jnp.ones((sub_rows + 1,), jnp.float32), -jnp.ones((sub_rows - 1,), jnp.float32)]
    )[:, None]
    keep_rows = (index_row > 0).astype(jnp.float32)[:, None]

    def transform(stacked):
        rows_data = stacked.reshape(-1, sub_rows, channels)
        spectra = jnp.einsum(
            "fs,ksc->kfc", forward_upper, rows_data, preferred_element_type=jnp.float32
        )
        spectra = spectra + jnp.einsum(
            "fs,ksc->kfc", forward_lower, rows_data, preferred_element_type=jnp.float32
        )
        return spectra.reshape(stacked.shape[0], SUBS, size_n, channels)

    def pair_sum(grad_spec, lag_stack, offset):
        later_spec = lax.slice_in_dim(lag_stack, offset + 1, offset + 1 + SUBS, axis=1)
        earlier = lax.slice_in_dim(lag_stack, offset, offset + SUBS, axis=1)
        factor = conj_sign * (later_spec + parity * earlier)
        grad_real = grad_spec[None, :, :sub_rows]
        grad_imag = grad_spec[None, :, sub_rows:]
        coef_real = factor[:, :, :sub_rows]
        coef_imag = factor[:, :, sub_rows:]
        imag_product = grad_imag * coef_imag
        product_real = grad_real * coef_real - keep_rows * imag_product
        product_imag = (
            keep_rows * (grad_real * coef_imag + grad_imag * coef_real)
            + (1.0 - keep_rows) * imag_product
        )
        return jnp.concatenate(
            [jnp.sum(product_real, axis=1), jnp.sum(product_imag, axis=1)], axis=1
        )

    def fetch_blocks(loop_step, grad_block):
        return (grad_block, spread(jnp.stack([filt, inner]), "seq", loop_step))

    def move_block(grad_block):
        return shifted(grad_block, "seq", -1)

    def contribute(loop_step, grad_block, previous, totals):
        grad_now, lag_pair = fetch_blocks(loop_step, grad_block)
        spectra = transform(jnp.concatenate([grad_now[None], lag_pair], axis=0))
        current = spectra[1:]
        lag_stack = jnp.concatenate([previous, current], axis=1)
        pair_terms = jnp.stack(
            [pair_sum(spectra[0], lag_stack, SUBS - 1 - which) for which in range(SUBS)], axis=1
        )
        return (current, totals + pair_terms)

    previous = jnp.zeros((2, SUBS, size_n, channels), jnp.float32)
    totals = jnp.zeros((2, SUBS, size_n, channels), jnp.float32)
    previous, totals = contribute(jnp.int32(0), grad_conv, previous, totals)

    def advance(loop_step, loop_carry):
        grad_block, previous, totals = loop_carry
        grad_block = move_block(grad_block)
        previous, totals = contribute(loop_step, grad_block, previous, totals)
        return (grad_block, previous, totals)

    loop_carry = lax.fori_loop(1, seq_count, advance, (grad_conv, previous, totals))
    spectra_out = loop_carry[2].reshape(2 * SUBS, size_n, channels)
    values = jnp.einsum(
        "nf,kfc->knc",
        inverse_matrix,
        spectra_out,
        precision=lax.Precision.HIGHEST,
        preferred_element_type=jnp.float32,
    )
    values = values.reshape(2, block_rows, channels)
    return (values[0].astype(jnp.bfloat16), values[1])


def solution(mesh):
    placed = (
        P("seq", "chan"),
        P("chan", None),
        P("seq", "chan"),
        P("seq", "chan"),
        P("seq", "chan"),
    )
    return jax.shard_map(
        body,
        mesh=mesh,
        in_specs=placed,
        out_specs=(P("seq", "chan"), P("seq", "chan")),
        check_vma=False,
    )
```

profile of v0, /device:TPU:0, one launch (start us, length us, event | category | flops | bytes accessed | tf_op | source)
XLA Modules:
  0.0 287.5 jit_solution(11338532694955231238)
XLA Ops:
  8.8 1.7 pad_maximum_fusion.4
  14.7 123.5 %all-gather.2.cloned.1.call-done = bf16[512,8192]{1,0:T(8,128)(2,1)} async-done(((bf16[512,1024]{1,0:T(8,128)(2,1)}), bf16[512,8192]{1,0:T(8,128)(2,1)}) %all-gather.2.cloned.1.call-update) | async-done | bytes 8388624 | tf_op jit(solution)/shard_map/all_gather | solution.py:34
  138.2 5.7 %fusion.11 = bf16[512,128]{1,0:T(8,128)(2,1)S(1)} fusion(bf16[512,8192]{1,0:T(8,128)(2,1)} %all-gather.2.cloned.1.call-done, bf16[128,8192]{1,0:T(8,128)(2,1)S(1)} %copy-done, bf16[512,128]{1,0:T(8,128)(2,1)S(1)} %copy-done.11), kind=kOutput, calls=%fused_computation.46 | convolution fusion | flops 1073938432 | bytes 10747904 | tf_op jit(solution)/shard_map/td,cd->tc/dot_general | solution.py:32
  148.0 127.6 %while.23 = (s32[]{:T(128)}, bf16[512,128]{1,0:T(8,128)(2,1)}, f32[2,4,256,128]{2,3,1,0:T(8,128)}, f32[2,4,256,128]{2,3,0,1:T(8,128)S(1)}, bf16[2,512,128]{2,1,0...) while((s32[]{:T(128)}, bf16[512,128]{1,0:T(8,128)(2,1)}, ...), condition=%wide.region_19.20_spmd.clone.clone, body=%wide.region_9.19_spmd.clone.clone.sunk | while | flops 213975680 | bytes 36311328 | solution.py:110
  148.1 1.3 collective-permute-start
  150.2 1.4 collective-permute-done
  151.6 30.7 %all-reduce.6.cloned.1.call-done = bf16[2,512,128]{2,1,0:T(8,128)(2,1)} async-done(((bf16[2,512,128]{2,1,0:T(8,128)(2,1)}), bf16[2,512,128]{2,1,0:T(8,128)(2,1)}) %all-reduce.6.cloned.1.call-update) | async-done | bytes 262160 | tf_op jit(solution)/shard_map/while/body/eval_jaxpr/psum | solution.py:12
  182.3 1.0 pad_maximum_fusion.8
  183.3 1.2 fusion.63
  185.1 1.1 copy-done.2
  189.5 1.3 collective-permute-start
  191.6 1.4 collective-permute-done
  192.9 32.6 %all-reduce.6.cloned.1.call-done = bf16[2,512,128]{2,1,0:T(8,128)(2,1)} async-done(((bf16[2,512,128]{2,1,0:T(8,128)(2,1)}), bf16[2,512,128]{2,1,0:T(8,128)(2,1)}) %all-reduce.6.cloned.1.call-update) | async-done | bytes 262160 | tf_op jit(solution)/shard_map/while/body/eval_jaxpr/psum | solution.py:12
  225.5 1.0 pad_maximum_fusion.8
  226.5 1.2 fusion.63
  228.3 1.1 copy-done.2
  232.7 1.3 collective-permute-start
  234.8 1.4 collective-permute-done
  236.2 32.3 %all-reduce.6.cloned.1.call-done = bf16[2,512,128]{2,1,0:T(8,128)(2,1)} async-done(((bf16[2,512,128]{2,1,0:T(8,128)(2,1)}), bf16[2,512,128]{2,1,0:T(8,128)(2,1)}) %all-reduce.6.cloned.1.call-update) | async-done | bytes 262160 | tf_op jit(solution)/shard_map/while/body/eval_jaxpr/psum | solution.py:12
  268.4 1.0 pad_maximum_fusion.8
  269.4 1.2 fusion.63
  271.2 1.1 copy-done.2
  275.7 1.3 copy.19
  277.0 1.9 convolution_bitcast_fusion
  (108 shorter events, 23.9 us)
Async XLA Ops:
  8.0 130.2 %copy-start = (bf16[128,8192]{1,0:T(8,128)(2,1)S(1)}, bf16[128,8192]{1,0:T(8,128)(2,1)}, u32[]{:S(2)}) copy-start(bf16[128,8192]{1,0:T(8,128)(2,1)} %param.12) | copy-start | bytes 6291460
  8.0 130.2 %copy-start.11 = (bf16[512,128]{1,0:T(8,128)(2,1)S(1)}, bf16[512,128]{1,0:T(8,128)(2,1)}, u32[]{:S(2)}) copy-start(bf16[512,128]{1,0:T(8,128)(2,1)} %param.13) | copy-start | bytes 393220
  8.0 130.2 %all-gather.2.cloned.1.call-start = ((), (), s32[]{:S(2)}) async-start(), calls=%async_computation | async-start | bytes 9437184 | tf_op jit(solution)/shard_map/all_gather | solution.py:34
  8.8 135.2 %all-reduce.4.cloned.1.call-start = ((), (), s32[]{:S(2)}) async-start(), calls=%async_computation.1 | async-start | bytes 524288 | tf_op jit(solution)/shard_map/psum | solution.py:12
  13.9 0.6 copy-start.6
  14.6 130.4 %copy-start.3 = (bf16[256,128]{1,0:T(8,128)(2,1)}, bf16[256,128]{1,0:T(8,128)(2,1)S(1)}, u32[]{:S(2)}) copy-start(bf16[256,128]{1,0:T(8,128)(2,1)S(1)} %fusion.14) | copy-start | bytes 196612
  14.6 130.8 %copy-start.5 = (bf16[256,128]{1,0:T(8,128)(2,1)}, bf16[256,128]{1,0:T(8,128)(2,1)S(1)}, u32[]{:S(2)}) copy-start(bf16[256,128]{1,0:T(8,128)(2,1)S(1)} %subtract_convert_fusion) | copy-start | bytes 196612
  144.0 1.9 copy-start.9
  145.8 0.7 copy-start.10
  146.0 1.0 copy-start.1
  148.1 34.2 %all-reduce.6.cloned.1.call-start = ((), (), s32[]{:S(2)}) async-start(), calls=%async_computation.2 | async-start | bytes 524288 | tf_op jit(solution)/shard_map/while/body/eval_jaxpr/psum | solution.py:12
  148.1 3.5 %collective-permute-start = (bf16[512,128]{1,0:T(8,128)(2,1)}, bf16[512,128]{1,0:T(8,128)(2,1)S(1)}, u32[]{:S(2)}, u32[]{:S(2)}) collective-permute-start(bf16[512,128]{1,0:T(8,128)(2,1)} %get-tuple-element.535), channel_id=1, source_target_pairs={{8,0},{16,8},{24,16},{9,1},{17,9},{25,17},{10,2},{18,10},{26,18},{... | collective-permute-start | bytes 393224 | tf_op jit(solution)/shard_map/while/body/eval_jaxpr/ppermute | solution.py:18
  182.3 2.3 copy-start.4
  184.9 1.2 copy-start.2
  189.5 36.0 %all-reduce.6.cloned.1.call-start = ((), (), s32[]{:S(2)}) async-start(), calls=%async_computation.2 | async-start | bytes 524288 | tf_op jit(solution)/shard_map/while/body/eval_jaxpr/psum | solution.py:12
  189.5 3.4 %collective-permute-start = (bf16[512,128]{1,0:T(8,128)(2,1)}, bf16[512,128]{1,0:T(8,128)(2,1)S(1)}, u32[]{:S(2)}, u32[]{:S(2)}) collective-permute-start(bf16[512,128]{1,0:T(8,128)(2,1)} %get-tuple-element.535), channel_id=1, source_target_pairs={{8,0},{16,8},{24,16},{9,1},{17,9},{25,17},{10,2},{18,10},{26,18},{... | collective-permute-start | bytes 393224 | tf_op jit(solution)/shard_map/while/body/eval_jaxpr/ppermute | solution.py:18
  225.5 2.3 copy-start.4
  228.2 1.2 copy-start.2
  232.7 35.7 %all-reduce.6.cloned.1.call-start = ((), (), s32[]{:S(2)}) async-start(), calls=%async_computation.2 | async-start | bytes 524288 | tf_op jit(solution)/shard_map/while/body/eval_jaxpr/psum | solution.py:12
  232.7 3.4 %collective-permute-start = (bf16[512,128]{1,0:T(8,128)(2,1)}, bf16[512,128]{1,0:T(8,128)(2,1)S(1)}, u32[]{:S(2)}, u32[]{:S(2)}) collective-permute-start(bf16[512,128]{1,0:T(8,128)(2,1)} %get-tuple-element.535), channel_id=1, source_target_pairs={{8,0},{16,8},{24,16},{9,1},{17,9},{25,17},{10,2},{18,10},{26,18},{... | collective-permute-start | bytes 393224 | tf_op jit(solution)/shard_map/while/body/eval_jaxpr/ppermute | solution.py:18
  268.4 2.3 copy-start.4
  271.1 1.2 copy-start.2
  275.7 1.3 copy-start.7
  275.7 1.3 copy-start.8
Sparse Core Ops, SparseCore 0:
  11.0 127.1 all-gather.1
  151.8 30.4 all-reduce.5
  193.2 32.2 all-reduce.5
  236.1 32.2 all-reduce.5
Sparse Core Ops, SparseCore 1:
  12.1 34.7 all-reduce.3
where the time goes:
time: 288 us; the launch traced here: 287 us
  waiting for transfers between devices  224 us (78%)
  other arithmetic  17.4 us (6%)
  between operations  15.4 us (5%)
  matrix products  13.3 us (5%)
  local copies, waits for them, and re-layouts  13 us (5%)
  starting transfers between devices  3.98 us (1%)
    all_gather x1, waiting for transfers between devices, body(): lax.all_gather(d_out, 'chan', axis=1, tiled=True)  124 us
    psum x4, waiting for transfers between devices, spread(): return lax.psum(block, axis)  95.5 us
    while x18, local copies, waits for them, and re-layouts  8.26 us
  transfers between devices with their start and end apart: 8, of which 7 were waited for; matrix products, arithmetic and copies ran while one was open for 5% of the time, Pallas kernels for 0%

commit v1 on v0

--- a/solution.py
+++ b/solution.py
@@ -9,7 +9,7 @@
 
 def spread(block, axis, holder):
     block = jnp.where(lax.axis_index(axis) == holder, block, jnp.zeros_like(block))
-    return lax.psum(block, axis)
+    return jnp.sum(lax.all_gather(block, axis), axis=0)
 
 
 def shifted(block, axis, distance):

time: 288 us -> 257 us (0.89)
  waiting for transfers between devices: 224 us -> 190 us
    psum x4 -> x0, waiting for transfers between devices: 95.5 us -> none  [spread(): return lax.psum(block, axis)]
    all_gather x0 -> x4, waiting for transfers between devices: none -> 57.6 us  [spread(): return jnp.sum(lax.all_gather(block, axis), axis=0)]
    reduce_sum x0 -> x4, other arithmetic: none -> 5.86 us  [spread(): return jnp.sum(lax.all_gather(block, axis), axis=0)]
    concatenate x4, other arithmetic: 4.06 us -> 0.15 us  [contribute(): spectra = transform(jnp.concatenate([grad_now[None], lag_pair], axis=0))]
    while x18 -> x30, local copies, waits for them, and re-layouts: 8.26 us -> 10.2 us
  transfers between devices with their start and end apart: 8 -> 8, of which waited for: 7 -> 8; matrix products, arithmetic and copies ran while one was open for 5% -> 3% of each run, Pallas kernels for 0% -> 0%
where the time goes in v1:
time: 257 us; the launch traced here: 256 us
  waiting for transfers between devices  190 us (74%)
  other arithmetic  19.7 us (8%)
  local copies, waits for them, and re-layouts  14.7 us (6%)
  between operations  14 us (5%)
  matrix products  13.3 us (5%)
  starting transfers between devices  4 us (2%)
    all_gather x1, waiting for transfers between devices, body(): lax.all_gather(d_out, 'chan', axis=1, tiled=True)  125 us
    all_gather x4, waiting for transfers between devices, spread(): return jnp.sum(lax.all_gather(block, axis), axis=0)  57.6 us
    while x30, local copies, waits for them, and re-layouts  10.2 us
    ppermute x3, waiting for transfers between devices, shifted(): return lax.ppermute(block, axis, route)  6.39 us
    reduce_sum x4, other arithmetic, spread(): return jnp.sum(lax.all_gather(block, axis), axis=0)  5.86 us
    dot_general x1, matrix products, body(): jnp.einsum('td,cd->tc', lax.all_gather(d_out, 'chan', axis=1, tiled=True)...  5.71 us
  transfers between devices with their start and end apart: 8, of which 8 were waited for; matrix products, arithmetic and copies ran while one was open for 3% of the time, Pallas kernels for 0%

profile of v1, /device:TPU:0, one launch (start us, length us, event | category | flops | bytes accessed | tf_op | source)
XLA Modules:
  0.0 256.1 jit_solution(7900339329332616735)
XLA Ops:
  7.2 1.9 pad_maximum_fusion.4
  13.7 15.8 %all-gather.6.cloned.1.call-done = bf16[4,2,512,128]{3,2,1,0:T(8,128)(2,1)} async-done(((bf16[1,2,512,128]{3,2,1,0:T(8,128)(2,1)}), bf16[4,2,512,128]{3,2,1,0:T(8,128)(2,1)}) %all-gather.6.cloned.1.call-update) | async-done | bytes 1048592 | tf_op jit(solution)/shard_map/all_gather | solution.py:12
  29.6 1.5 reduce_sum.226
  31.0 125.2 %all-gather.4.cloned.1.call-done = bf16[512,8192]{1,0:T(8,128)(2,1)} async-done(((bf16[512,1024]{1,0:T(8,128)(2,1)}), bf16[512,8192]{1,0:T(8,128)(2,1)}) %all-gather.4.cloned.1.call-update) | async-done | bytes 8388624 | tf_op jit(solution)/shard_map/all_gather | solution.py:34
  156.3 5.7 %fusion.11 = bf16[512,128]{1,0:T(8,128)(2,1)S(1)} fusion(bf16[512,8192]{1,0:T(8,128)(2,1)} %all-gather.4.cloned.1.call-done, bf16[128,8192]{1,0:T(8,128)(2,1)S(1)} %copy-done, bf16[512,128]{1,0:T(8,128)(2,1)S(1)} %copy-done.13), kind=kOutput, calls=%fused_computation.46 | convolution fusion | flops 1073938432 | bytes 10747904 | tf_op jit(solution)/shard_map/td,cd->tc/dot_general | solution.py:32
  165.1 79.8 %while.23 = (s32[]{:T(128)}, bf16[512,128]{1,0:T(8,128)(2,1)}, f32[2,4,256,128]{2,3,1,0:T(8,128)}, f32[2,4,256,128]{2,3,0,1:T(8,128)S(1)}, bf16[1,2,512,128]{3,2...) while((s32[]{:T(128)}, bf16[512,128]{1,0:T(8,128)(2,1)}, ...), condition=%wide.region_19.20_spmd.clone.clone, body=%wide.region_9.19_spmd.clone.clone.sunk | while | flops 214237824 | bytes 42078560 | solution.py:110
  165.9 1.3 collective-permute-start
  167.2 2.1 collective-permute-done
  170.0 12.9 %all-gather.8.cloned.1.call-done = bf16[4,2,512,128]{3,2,1,0:T(8,128)(2,1)} async-done(((bf16[1,2,512,128]{3,2,1,0:T(8,128)(2,1)}), bf16[4,2,512,128]{3,2,1,0:T(8,128)(2,1)}) %all-gather.8.cloned.1.call-update) | async-done | bytes 1048592 | tf_op jit(solution)/shard_map/while/body/eval_jaxpr/all_gather | solution.py:12
  182.9 1.5 reduce_sum.272
  184.5 1.2 fusion.63
  191.5 1.3 collective-permute-start
  192.8 2.1 collective-permute-done
  195.6 14.4 %all-gather.8.cloned.1.call-done = bf16[4,2,512,128]{3,2,1,0:T(8,128)(2,1)} async-done(((bf16[1,2,512,128]{3,2,1,0:T(8,128)(2,1)}), bf16[4,2,512,128]{3,2,1,0:T(8,128)(2,1)}) %all-gather.8.cloned.1.call-update) | async-done | bytes 1048592 | tf_op jit(solution)/shard_map/while/body/eval_jaxpr/all_gather | solution.py:12
  210.0 1.5 reduce_sum.272
  211.6 1.2 fusion.63
  218.6 1.3 collective-permute-start
  219.9 2.1 collective-permute-done
  222.7 14.4 %all-gather.8.cloned.1.call-done = bf16[4,2,512,128]{3,2,1,0:T(8,128)(2,1)} async-done(((bf16[1,2,512,128]{3,2,1,0:T(8,128)(2,1)}), bf16[4,2,512,128]{3,2,1,0:T(8,128)(2,1)}) %all-gather.8.cloned.1.call-update) | async-done | bytes 1048592 | tf_op jit(solution)/shard_map/while/body/eval_jaxpr/all_gather | solution.py:12
  237.1 1.5 reduce_sum.272
  238.7 1.2 fusion.63
  240.5 1.1 copy-done.2
  244.9 1.3 copy.19
  246.2 1.9 convolution_bitcast_fusion
  (124 shorter events, 27.1 us)
Async XLA Ops:
  7.2 149.1 %copy-start = (bf16[128,8192]{1,0:T(8,128)(2,1)S(1)}, bf16[128,8192]{1,0:T(8,128)(2,1)}, u32[]{:S(2)}) copy-start(bf16[128,8192]{1,0:T(8,128)(2,1)} %param.12) | copy-start | bytes 6291460
  7.2 22.4 %all-gather.6.cloned.1.call-start = ((), (), s32[]{:S(2)}) async-start(), calls=%async_computation.1 | async-start | bytes 1310720 | tf_op jit(solution)/shard_map/all_gather | solution.py:12
  7.2 149.0 %copy-start.13 = (bf16[512,128]{1,0:T(8,128)(2,1)S(1)}, bf16[512,128]{1,0:T(8,128)(2,1)}, u32[]{:S(2)}) copy-start(bf16[512,128]{1,0:T(8,128)(2,1)} %param.13) | copy-start | bytes 393220
  9.1 147.1 %all-gather.4.cloned.1.call-start = ((), (), s32[]{:S(2)}) async-start(), calls=%async_computation | async-start | bytes 9437184 | tf_op jit(solution)/shard_map/all_gather | solution.py:34
  12.7 149.3 %copy-start.5 = (bf16[256,128]{1,0:T(8,128)(2,1)}, bf16[256,128]{1,0:T(8,128)(2,1)S(1)}, u32[]{:S(2)}) copy-start(bf16[256,128]{1,0:T(8,128)(2,1)S(1)} %fusion.14) | copy-start | bytes 196612
  13.7 148.7 %copy-start.7 = (bf16[256,128]{1,0:T(8,128)(2,1)}, bf16[256,128]{1,0:T(8,128)(2,1)S(1)}, u32[]{:S(2)}) copy-start(bf16[256,128]{1,0:T(8,128)(2,1)S(1)} %subtract_convert_fusion) | copy-start | bytes 196612
  163.0 1.0 copy-start.1
  165.1 5.0 %copy-start.3 = (bf16[1,2,512,128]{3,2,1,0:T(8,128)(2,1)}, bf16[1,2,512,128]{3,2,1,0:T(8,128)(2,1)S(1)}, u32[]{:S(2)}) copy-start(bf16[1,2,512,128]{3,2,1,0:T(8,128)(2,1)S(1)} %get-tuple-element.563) | copy-start | bytes 786436 | tf_op jit(solution)/shard_map/while
  165.1 17.9 %all-gather.8.cloned.1.call-start = ((), (), s32[]{:S(2)}) async-start(), calls=%async_computation.2 | async-start | bytes 1310720 | tf_op jit(solution)/shard_map/while/body/eval_jaxpr/all_gather | solution.py:12
  165.9 3.5 %collective-permute-start = (bf16[512,128]{1,0:T(8,128)(2,1)}, bf16[512,128]{1,0:T(8,128)(2,1)S(1)}, u32[]{:S(2)}, u32[]{:S(2)}) collective-permute-start(bf16[512,128]{1,0:T(8,128)(2,1)} %get-tuple-element.548), channel_id=1, source_target_pairs={{8,0},{16,8},{24,16},{9,1},{17,9},{25,17},{10,2},{18,10},{26,18},{... | collective-permute-start | bytes 393224 | tf_op jit(solution)/shard_map/while/body/eval_jaxpr/ppermute | solution.py:18
  184.4 1.3 copy-start.6
  186.1 1.2 copy-start.2
  190.7 4.9 %copy-start.3 = (bf16[1,2,512,128]{3,2,1,0:T(8,128)(2,1)}, bf16[1,2,512,128]{3,2,1,0:T(8,128)(2,1)S(1)}, u32[]{:S(2)}) copy-start(bf16[1,2,512,128]{3,2,1,0:T(8,128)(2,1)S(1)} %get-tuple-element.563) | copy-start | bytes 786436 | tf_op jit(solution)/shard_map/while
  190.7 19.4 %all-gather.8.cloned.1.call-start = ((), (), s32[]{:S(2)}) async-start(), calls=%async_computation.2 | async-start | bytes 1310720 | tf_op jit(solution)/shard_map/while/body/eval_jaxpr/all_gather | solution.py:12
  191.5 3.5 %collective-permute-start = (bf16[512,128]{1,0:T(8,128)(2,1)}, bf16[512,128]{1,0:T(8,128)(2,1)S(1)}, u32[]{:S(2)}, u32[]{:S(2)}) collective-permute-start(bf16[512,128]{1,0:T(8,128)(2,1)} %get-tuple-element.548), channel_id=1, source_target_pairs={{8,0},{16,8},{24,16},{9,1},{17,9},{25,17},{10,2},{18,10},{26,18},{... | collective-permute-start | bytes 393224 | tf_op jit(solution)/shard_map/while/body/eval_jaxpr/ppermute | solution.py:18
  211.5 1.3 copy-start.6
  213.2 1.2 copy-start.2
  217.8 4.9 %copy-start.3 = (bf16[1,2,512,128]{3,2,1,0:T(8,128)(2,1)}, bf16[1,2,512,128]{3,2,1,0:T(8,128)(2,1)S(1)}, u32[]{:S(2)}) copy-start(bf16[1,2,512,128]{3,2,1,0:T(8,128)(2,1)S(1)} %get-tuple-element.563) | copy-start | bytes 786436 | tf_op jit(solution)/shard_map/while
  217.8 19.4 %all-gather.8.cloned.1.call-start = ((), (), s32[]{:S(2)}) async-start(), calls=%async_computation.2 | async-start | bytes 1310720 | tf_op jit(solution)/shard_map/while/body/eval_jaxpr/all_gather | solution.py:12
  218.6 3.5 %collective-permute-start = (bf16[512,128]{1,0:T(8,128)(2,1)}, bf16[512,128]{1,0:T(8,128)(2,1)S(1)}, u32[]{:S(2)}, u32[]{:S(2)}) collective-permute-start(bf16[512,128]{1,0:T(8,128)(2,1)} %get-tuple-element.548), channel_id=1, source_target_pairs={{8,0},{16,8},{24,16},{9,1},{17,9},{25,17},{10,2},{18,10},{26,18},{... | collective-permute-start | bytes 393224 | tf_op jit(solution)/shard_map/while/body/eval_jaxpr/ppermute | solution.py:18
  238.6 1.3 copy-start.6
  240.3 1.2 copy-start.2
  244.9 1.3 copy-start.9
  244.9 1.3 copy-start.10
  (6 other events, 5.0 us)
Sparse Core Ops, SparseCore 0:
  10.1 19.4 all-gather.5
  31.8 124.4 all-gather.3
  168.0 14.8 all-gather.7
  193.3 16.6 all-gather.7
  220.4 16.6 all-gather.7
